TPU v7x, 512 devices: a whole 4x4x16 slice. The times are simulated.
512 devices in a mesh: buyers: 32 (over y, z_lo), goods: 16 (over x, z_hi, core).
Axes of the slice: x: 4, y: 4, z: 16 (z_hi: 2, z_lo: 8; z = z_hi * 8 + z_lo), core: 2. Of those that a mesh axis runs over, the one named last changes fastest.
Arguments:
- buyer_hidden: bfloat16 [40960, 1024], P('buyers', 'goods'), may hold values from -6 to 6
- goods_hidden: bfloat16 [32768, 1024], P('goods', 'buyers'), may hold values from -6 to 6
- buyer_proj: bfloat16 [1024, 128], replicated, may hold values from -0.1875 to 0.1875
- goods_proj: bfloat16 [1024, 128], replicated, may hold values from -0.1875 to 0.1875
- endowment: float32 [40960], P('buyers'), may hold values from 0.5 to 4
Outputs:
- prices: float32 [32768], P('goods')
- utility: float32 [40960], P('buyers')
All inputs are finite; a program needn't handle non-finite values.
Results may differ from a plain program's by a relative error of at most 0.0003.
The roundings to bfloat16 on the way count: a program that leaves them out, or rounds other values in their place, can miss the bound.
Values may be sent and summed in bfloat16 or wider, within the bound.
No kernel may reach another device: no remote copies, remote signals or barrier semaphores. Data moves between devices by JAX's collectives and lax.ppermute only.
A program may use at most 64 MiB of HBM per device.

v0:
```python
import jax
import jax.numpy as jnp
from jax import lax
from jax.sharding import PartitionSpec as P

E = 128
ITERS = 3


def per_device(buyer_hidden, goods_hidden, buyer_proj, goods_proj, endowment):
    proj_rows = buyer_proj
    buyer_sum = jnp.dot(
        lax.all_gather(buyer_hidden, "goods", axis=1, tiled=True),
        proj_rows,
        preferred_element_type=jnp.float32,
    )
    proj_rows = goods_proj
    goods_sum = jnp.dot(
        lax.all_gather(goods_hidden, "buyers", axis=1, tiled=True),
        proj_rows,
        preferred_element_type=jnp.float32,
    )
    buyer_emb = buyer_sum.astype(jnp.bfloat16)
    goods_emb = goods_sum.astype(jnp.bfloat16)
    scores = lax.dot_general(
        buyer_emb, goods_emb, (((1,), (1,)), ((), ())), preferred_element_type=jnp.float32
    )
    values = jax.nn.softplus(scores * E ** (-0.5)).astype(jnp.bfloat16)
    spread = lax.psum(jnp.sum(values, axis=1, dtype=jnp.float32), "goods")
    bid_block = (endowment / spread)[:, None] * values
    prices = spread
    utility = spread
    for repeat in range(ITERS):
        prices = lax.psum(jnp.sum(bid_block, 0), "buyers")
        shares = bid_block / prices[None, :]
        utility = lax.psum(jnp.sum(values * shares, 1), "goods")
        if repeat + 1 < ITERS:
            bid_block = (endowment / utility)[:, None] * values * shares
    return (prices, utility)


def solution(mesh):
    placed = (P("buyers", "goods"), P("goods", "buyers"), P(), P(), P("buyers"))
    return jax.shard_map(
        per_device, mesh=mesh, in_specs=placed, out_specs=(P("goods"), P("buyers")), check_vma=False
    )
```

profile of v0, /device:TPU:1, one launch (start us, length us, event | category | flops | bytes accessed | tf_op | source)
XLA Modules:
  0.0 1007.6 jit_solution(11603073471808425015)
XLA Ops:
  7.2 0.0 copy-start
  7.2 0.0 all-gather.5.cloned.1.call-start
  7.2 0.7 all-gather.5.cloned.1.call-update
  7.9 0.0 all-gather.3.cloned.1.call-start
  8.0 0.7 all-gather.3.cloned.1.call-update
  8.7 223.9 %all-gather.5.cloned.1.call-done = bf16[2048,1024]{0,1:T(8,128)(2,1)} async-done(((bf16[2048,32]{0,1:T(8,128)(2,1)}), bf16[2048,1024]{0,1:T(8,128)(2,1)}) %all-gather.5.cloned.1.call-update) | async-done | bytes 4194320 | tf_op jit(solution)/shard_map/all_gather | solution.py:19
  232.5 3.5 convolution_convert_fusion
  236.1 0.0 copy-start.1
  236.1 117.2 %all-gather.3.cloned.1.call-done = bf16[1280,1024]{0,1:T(8,128)(2,1)} async-done(((bf16[1280,64]{0,1:T(8,128)(2,1)}), bf16[1280,1024]{0,1:T(8,128)(2,1)}) %all-gather.3.cloned.1.call-update) | async-done | bytes 2621456 | tf_op jit(solution)/shard_map/all_gather | solution.py:13
  353.3 0.0 copy-done
  353.3 11.8 %convert_reduce_fusion = (f32[1280]{0:T(1024)S(1)}, bf16[1280,2048]{1,0:T(8,128)(2,1)}) fusion(bf16[2048,128]{1,0:T(8,128)(2,1)S(1)} %convolution_convert_fusion, bf16[1280,1024]{0,1:T(8,128)(2,1)} %all-gather.3.cloned.1.call-done, bf16[1024,128]{1,0:T(8,128)(2,1)S(1)} %copy-done), kind=kOutput, calls=%fused_computation.7 | convolution fusion | flops 1033009920 | bytes 8655872 | tf_op jit(solution)/shard_map/dot_general | solution.py:25
  365.2 62.1 %psum.49 = f32[1280]{0:T(1024)S(1)} all-reduce(f32[1280]{0:T(1024)S(1)} %get-tuple-element.2), channel_id=1, replica_groups=mesh['buyers'=32,'goods'=16] {'goods'}, use_global_device_ids=true, to_apply=%region_1.2 | all-reduce | flops 1280 | bytes 10240 | tf_op jit(solution)/shard_map/psum | solution.py:29
  427.3 0.0 copy-done.1
  427.3 3.6 fusion.1
  430.9 101.5 %psum.50 = f32[2048]{0:T(1024)S(1)} all-reduce(f32[2048]{0:T(1024)S(1)} %fusion.1), channel_id=1, replica_groups=mesh['buyers'=32,'goods'=16] {'buyers'}, use_global_device_ids=true, to_apply=%region_3.4 | all-reduce | flops 2048 | bytes 16384 | tf_op jit(solution)/shard_map/psum | solution.py:34
  532.3 4.4 fusion.2
  536.7 84.0 %psum.51 = f32[1280]{0:T(1024)S(1)} all-reduce(f32[1280]{0:T(1024)S(1)} %fusion.2), channel_id=1, replica_groups=mesh['buyers'=32,'goods'=16] {'goods'}, use_global_device_ids=true, to_apply=%region_5.6 | all-reduce | flops 1280 | bytes 10240 | tf_op jit(solution)/shard_map/psum | solution.py:36
  620.7 4.7 fusion.9
  625.5 101.0 %psum.52 = f32[2048]{0:T(1024)S(1)} all-reduce(f32[2048]{0:T(1024)S(1)} %fusion.9), channel_id=1, replica_groups=mesh['buyers'=32,'goods'=16] {'buyers'}, use_global_device_ids=true, to_apply=%region_7.8 | all-reduce | flops 2048 | bytes 16384 | tf_op jit(solution)/shard_map/psum | solution.py:34
  726.5 4.9 fusion.4
  731.4 76.3 %psum.53 = f32[1280]{0:T(1024)S(1)} all-reduce(f32[1280]{0:T(1024)S(1)} %fusion.4), channel_id=1, replica_groups=mesh['buyers'=32,'goods'=16] {'goods'}, use_global_device_ids=true, to_apply=%region_9.10 | all-reduce | flops 1280 | bytes 10240 | tf_op jit(solution)/shard_map/psum | solution.py:36
  807.7 6.5 fusion.8
  814.2 102.8 %psum.54 = f32[2048]{0:T(1024)S(1)} all-reduce(f32[2048]{0:T(1024)S(1)} %fusion.8), channel_id=1, replica_groups=mesh['buyers'=32,'goods'=16] {'buyers'}, use_global_device_ids=true, to_apply=%region_11.12 | all-reduce | flops 2048 | bytes 16384 | tf_op jit(solution)/shard_map/psum | solution.py:34
  917.0 0.0 copy-start.2
  917.0 6.5 fusion.6
  923.5 77.4 %psum.55 = f32[1280]{0:T(1024)} all-reduce(f32[1280]{0:T(1024)S(1)} %fusion.6), channel_id=1, replica_groups=mesh['buyers'=32,'goods'=16] {'goods'}, use_global_device_ids=true, to_apply=%region_13.14 | all-reduce | flops 1280 | bytes 10240 | tf_op jit(solution)/shard_map/psum | solution.py:36
  1000.8 0.0 copy-done.2
  (3 shorter events, 0.0 us)
Async XLA Ops:
  7.2 346.2 %copy-start = (bf16[1024,128]{1,0:T(8,128)(2,1)S(1)}, bf16[1024,128]{1,0:T(8,128)(2,1)}, u32[]{:S(2)}) copy-start(bf16[1024,128]{1,0:T(8,128)(2,1)} %param.7) | copy-start | bytes 786436
  7.2 225.4 %all-gather.5.cloned.1.call-start = ((), (), s32[]{:S(2)}) async-start(), calls=%async_computation.1 | async-start | bytes 4325376 | tf_op jit(solution)/shard_map/all_gather | solution.py:19
  7.9 345.4 %all-gather.3.cloned.1.call-start = ((), (), s32[]{:S(2)}) async-start(), calls=%async_computation | async-start | bytes 2785280 | tf_op jit(solution)/shard_map/all_gather | solution.py:13
  236.1 191.2 %copy-start.1 = (f32[1280]{0:T(1024)S(1)}, f32[1280]{0:T(1024)}, u32[]{:S(2)}) copy-start(f32[1280]{0:T(1024)} %param.9) | copy-start | bytes 15364
  917.0 83.8 %copy-start.2 = (f32[2048]{0:T(1024)}, f32[2048]{0:T(1024)S(1)}, u32[]{:S(2)}) copy-start(f32[2048]{0:T(1024)S(1)} %psum.54) | copy-start | bytes 24580
Sparse Core Ops, SparseCore 0:
  10.1 222.4 all-gather.4
  235.8 117.4 all-gather.2
where the time goes:
time: 1010 us
  blocking collectives  605 us (60%)
  waiting for transfers between devices  343 us (34%)
  other arithmetic  30.6 us (3%)
  matrix products  15.3 us (2%)
  between operations  14.2 us (1%)
    psum x3, blocking collectives, per_device(): prices = lax.psum(jnp.sum(bid_block, 0), 'buyers')  305 us
    psum x3, blocking collectives, per_device(): utility = lax.psum(jnp.sum(values * shares, 1), 'goods')  238 us
    all_gather x1, waiting for transfers between devices, per_device(): lax.all_gather(goods_hidden, 'buyers', axis=1, tiled=True)  224 us
    all_gather x1, waiting for transfers between devices, per_device(): lax.all_gather(buyer_hidden, 'goods', axis=1, tiled=True)  117 us
    psum x1, blocking collectives, per_device(): spread = lax.psum(jnp.sum(values, axis=1, dtype=jnp.float32), 'goods')  62.1 us
  transfers between devices with their start and end apart: 2, of which 2 were waited for; matrix products, arithmetic and copies ran while one was open for 0% of the time, Pallas kernels for 0%

commit v1 on v0

v1 whole, which is shorter than its diff:
```python
import jax
import jax.numpy as jnp
from jax import lax
from jax.sharding import Mesh, PartitionSpec as P

E = 128
ITERS = 3
FINE = (("y", 4), ("zl", 8), ("x", 4), ("zh", 2), ("c", 2))
PLANE = ("y", "x", "c")
RING = ("zh", "zl")


def exchange(x, axes):
    return lax.all_to_all(x, axes, 0, 0, tiled=True)


def spread_out(x, axes, n):
    return exchange(jnp.broadcast_to(x[None], (n,) + x.shape), axes)


def per_device(buyer_hidden, goods_hidden, buyer_proj, goods_proj, endowment):
    n_plane, n_ring = 32, 16
    rows = lax.all_to_all(buyer_hidden, ("x", "zh", "c"), 0, 1, tiled=True)
    buyer_own = jnp.dot(rows, buyer_proj, preferred_element_type=jnp.float32).astype(jnp.bfloat16)
    rows = lax.all_to_all(goods_hidden, ("y", "zl"), 0, 1, tiled=True)
    goods_own = jnp.dot(rows, goods_proj, preferred_element_type=jnp.float32).astype(jnp.bfloat16)
    buyer_emb = spread_out(buyer_own, PLANE, n_plane).reshape(-1, E)
    goods_emb = spread_out(goods_own, RING, n_ring).reshape(-1, E)
    scores = lax.dot_general(
        buyer_emb, goods_emb, (((1,), (1,)), ((), ())), preferred_element_type=jnp.float32
    )
    values = jax.nn.softplus(scores * E ** (-0.5)).astype(jnp.bfloat16)
    nb, ng = values.shape

    mine = (lax.axis_index("x") * 4 + lax.axis_index("zh") * 2 + lax.axis_index("c")) * 80
    money = lax.dynamic_slice(endowment, (mine,), (80,))

    def goods_total(part):
        return jnp.sum(spread_out(part.reshape(-1, 128), PLANE, n_plane), 0).reshape(-1)

    def buyers_total(part):
        return jnp.sum(spread_out(part.reshape(-1, 128), RING, n_ring), 0).reshape(-1)

    part = jnp.sum(values, axis=1, dtype=jnp.float32)
    got = spread_out(jnp.concatenate([part, money, jnp.zeros((48,), jnp.float32)]).reshape(-1, 128), PLANE, n_plane)
    spread = jnp.sum(got[:, :20], 0).reshape(-1)
    money = got[:, 20, :80].reshape(-1)

    bid_block = (money / spread)[:, None] * values
    for repeat in range(ITERS):
        prices = buyers_total(jnp.sum(bid_block, 0))
        shares = bid_block / prices[None, :]
        part = jnp.sum(values * shares, 1)
        if repeat + 1 < ITERS:
            utility = goods_total(part)
            bid_block = (money / utility)[:, None] * values * shares
    half = lax.dynamic_slice(prices, (lax.axis_index("zh") * 512,), (512,))
    prices = spread_out(half.reshape(4, 128), ("y",), 4).reshape(-1)
    sent = jnp.broadcast_to(part.reshape(1, 4, 1, 5, 128), (2, 4, 8, 5, 128)).reshape(64, 5, 128)
    got = exchange(sent, ("zh", "y", "x", "c")).reshape(2, 32, 640)
    utility = jnp.sum(got, 1).reshape(2, 4, 160).transpose(1, 0, 2).reshape(-1)
    return (prices, utility)


def solution(mesh):
    fine = Mesh(mesh.devices.reshape([n for _, n in FINE]), [a for a, _ in FINE])
    buyers, goods = ("y", "zl"), ("x", "zh", "c")
    placed = (P(buyers, goods), P(goods, buyers), P(), P(), P(buyers))
    return jax.shard_map(
        per_device, mesh=fine, in_specs=placed, out_specs=(P(goods), P(buyers)), check_vma=False
    )
```

time: 1010 us -> 282 us (0.28)
  the two profiles are of different devices: /device:TPU:1 before, /device:TPU:33 now
where the time goes in v1:
time: 282 us; the launch traced here: 281 us
  waiting for transfers between devices  101 us (36%)
  blocking collectives  76.4 us (27%)
  starting transfers between devices  53 us (19%)
  other arithmetic  29.8 us (11%)
  local copies, waits for them, and re-layouts  10.7 us (4%)
  matrix products  9.46 us (3%)
    all_to_all x5, blocking collectives, exchange(): return lax.all_to_all(x, axes, 0, 0, tiled=True)  76.4 us
    all_to_all x5, waiting for transfers between devices, exchange(): return lax.all_to_all(x, axes, 0, 0, tiled=True)  67.1 us
    all_to_all x5, starting transfers between devices, exchange(): return lax.all_to_all(x, axes, 0, 0, tiled=True)  27.9 us
    all_to_all x1, waiting for transfers between devices, per_device(): rows = lax.all_to_all(buyer_hidden, ('x', 'zh', 'c'), 0, 1, tiled=True)  22.2 us
    all_to_all x1, starting transfers between devices, per_device(): rows = lax.all_to_all(buyer_hidden, ('x', 'zh', 'c'), 0, 1, tiled=True)  17.3 us
    reduce_sum x3, other arithmetic, per_device(): part = jnp.sum(values * shares, 1)  15.9 us
    reduce_sum x3, other arithmetic, per_device(): prices = buyers_total(jnp.sum(bid_block, 0))  13.6 us
    all_to_all x1, waiting for transfers between devices, per_device(): rows = lax.all_to_all(goods_hidden, ('y', 'zl'), 0, 1, tiled=True)  11.4 us
  transfers between devices with their start and end apart: 7, of which 6 were waited for; matrix products, arithmetic and copies ran while one was open for 3% of the time, Pallas kernels for 0%

profile of v1, /device:TPU:33, one launch (start us, length us, event | category | flops | bytes accessed | tf_op | source)
XLA Modules:
  0.0 280.9 jit_solution(4723974415362793196)
XLA Ops:
  0.6 0.0 copy-start
  0.6 0.0 copy-start.1
  0.7 1.4 all_to_all.58
  2.0 0.8 copy.23
  2.8 17.3 %all-to-all-start = ((bf16[16,80,64]{1,2,0:T(8,128)(2,1)}), bf16[16,80,64]{1,2,0:T(8,128)(2,1)S(1)}, u32[]{:S(2)}, u32[]{:S(2)}) async-start(bf16[16,80,64]{1,2,0:T(8,128)(2,1)} %copy.23), calls=%async_computation | async-start | bytes 524288 | tf_op jit(solution)/shard_map/all_to_all | solution.py:23
  20.1 1.2 all_to_all.63
  21.3 0.1 copy.35
  21.4 0.9 reshape.102
  22.3 22.2 %all-to-all-done = bf16[16,80,64]{1,2,0:T(8,128)(2,1)S(1)} async-done(((bf16[16,80,64]{1,2,0:T(8,128)(2,1)}), bf16[16,80,64]{1,2,0:T(8,128)(2,1)S(1)}, u32[]{:S(2)}, u32[]{:S(2)}) %all-to-all-start) | async-done | bytes 163872 | tf_op jit(solution)/shard_map/all_to_all | solution.py:23
  44.5 7.8 %all-to-all-start.2 = ((bf16[32,2,1024]{2,1,0:T(2,128)(2,1)}), bf16[32,2,1024]{2,1,0:T(2,128)(2,1)S(1)}, u32[]{:S(2)}, u32[]{:S(2)}) async-start(bf16[32,2,1024]{2,1,0:T(2,128)(2,1)} %reshape.102), calls=%async_computation.2 | async-start | bytes 262144 | tf_op jit(solution)/shard_map/all_to_all | solution.py:25
  52.3 0.0 copy-done
  52.3 0.2 convolution_convert_fusion
  52.5 11.4 %all-to-all-done.2 = bf16[32,2,1024]{2,1,0:T(2,128)(2,1)S(1)} async-done(((bf16[32,2,1024]{2,1,0:T(2,128)(2,1)}), bf16[32,2,1024]{2,1,0:T(2,128)(2,1)S(1)}, u32[]{:S(2)}, u32[]{:S(2)}) %all-to-all-start.2) | async-done | bytes 131104 | tf_op jit(solution)/shard_map/all_to_all | solution.py:25
  63.9 0.9 broadcast_in_dim.74
  64.9 6.0 %all-to-all-start.1 = ((bf16[32,80,128]{2,1,0:T(8,128)(2,1)}), bf16[32,80,128]{2,1,0:T(8,128)(2,1)S(1)}, u32[]{:S(2)}, u32[]{:S(2)}) async-start(bf16[32,80,128]{2,1,0:T(8,128)(2,1)} %broadcast_in_dim.74), calls=%async_computation.1 | async-start | bytes 1310720 | tf_op jit(solution)/shard_map/all_to_all | solution.py:14
  70.9 0.2 reshape.103
  71.1 0.0 copy-done.1
  71.1 0.2 convolution_convert_fusion.1
  71.4 12.5 %all-to-all-done.1 = bf16[32,80,128]{2,1,0:T(8,128)(2,1)S(1)} async-done(((bf16[32,80,128]{2,1,0:T(8,128)(2,1)}), bf16[32,80,128]{2,1,0:T(8,128)(2,1)S(1)}, u32[]{:S(2)}, u32[]{:S(2)}) %all-to-all-start.1) | async-done | bytes 655392 | tf_op jit(solution)/shard_map/all_to_all | solution.py:14
  83.8 0.7 broadcast_in_dim.75
  84.6 5.0 %all-to-all-start.3 = ((bf16[16,64,128]{2,1,0:T(8,128)(2,1)}), bf16[16,64,128]{2,1,0:T(8,128)(2,1)S(1)}, u32[]{:S(2)}, u32[]{:S(2)}) async-start(bf16[16,64,128]{2,1,0:T(8,128)(2,1)} %broadcast_in_dim.75), calls=%async_computation.3 | async-start | bytes 524288 | tf_op jit(solution)/shard_map/all_to_all | solution.py:14
  89.6 0.8 dynamic_slice.6
  90.3 17.2 %all-to-all-done.3 = bf16[16,64,128]{2,1,0:T(8,128)(2,1)S(1)} async-done(((bf16[16,64,128]{2,1,0:T(8,128)(2,1)}), bf16[16,64,128]{2,1,0:T(8,128)(2,1)S(1)}, u32[]{:S(2)}, u32[]{:S(2)}) %all-to-all-start.3) | async-done | bytes 262176 | tf_op jit(solution)/shard_map/all_to_all | solution.py:14
  107.5 9.0 %convert_reduce_fusion = (f32[2560]{0:T(1024)S(1)}, bf16[2560,1024]{0,1:T(8,128)(2,1)}) fusion(bf16[2560,128]{1,0:T(8,128)(2,1)S(1)} %bitcast.45, bf16[1024,128]{1,0:T(8,128)(2,1)S(1)} %bitcast.46), kind=kOutput, calls=%fused_computation.7 | convolution fusion | flops 697300480 | bytes 6170624 | tf_op jit(solution)/shard_map/dot_general | solution.py:29
  116.5 0.1 concatenate.3
  116.6 14.5 %all_to_all.88 = f32[32,21,128]{2,1,0:T(8,128)S(1)} all-to-all(f32[32,21,128]{2,1,0:T(8,128)S(1)} %broadcast_in_dim.78), channel_id=1, replica_groups=mesh['y'=4,'zl'=8,'x'=4,'zh'=2,'c'=2] {'y','x','c'}, dimensions={0} | all-to-all | bytes 688128 | tf_op jit(solution)/shard_map/all_to_all | solution.py:14
  131.2 0.1 slice_reduce_fusion.1
  131.2 0.1 reshape_squeeze.3
  131.4 3.6 %fusion.1 = f32[1024]{0:T(1024)S(1)} fusion(bf16[2560,1024]{0,1:T(8,128)(2,1)} %get-tuple-element.3, f32[2560]{0:T(1024)S(1)} %bitcast_divide_fusion.2), kind=kLoop, calls=%fused_computation.9 | loop fusion | flops 7863296 | bytes 5257216 | tf_op jit(solution)/shard_map/reduce_sum | solution.py:51
  134.9 16.8 %all_to_all.89 = f32[16,8,128]{2,1,0:T(8,128)S(1)} all-to-all(f32[16,8,128]{2,1,0:T(8,128)S(1)} %broadcast_in_dim.80), channel_id=1, replica_groups=mesh['y'=4,'zl'=8,'x'=4,'zh'=2,'c'=2] {'zh','zl'}, dimensions={0} | all-to-all | bytes 131072 | tf_op jit(solution)/shard_map/all_to_all | solution.py:14
  151.7 4.4 %fusion.2 = f32[2560]{0:T(1024)S(1)} fusion(bf16[2560,1024]{0,1:T(8,128)(2,1)} %get-tuple-element.3, f32[1024]{0:T(1024)S(1)} %bitcast.47, f32[2560]{0:T(1024)S(1)} %bitcast_divide_fusion.2), kind=kLoop, calls=%fused_computation.10 | loop fusion | flops 13104640 | bytes 5267456 | tf_op jit(solution)/shard_map/reduce_sum | solution.py:53
  156.2 15.4 %all_to_all.90 = f32[32,20,128]{2,1,0:T(8,128)S(1)} all-to-all(f32[32,20,128]{2,1,0:T(8,128)S(1)} %broadcast_in_dim.82), channel_id=1, replica_groups=mesh['y'=4,'zl'=8,'x'=4,'zh'=2,'c'=2] {'y','x','c'}, dimensions={0} | all-to-all | bytes 655360 | tf_op jit(solution)/shard_map/all_to_all | solution.py:14
  171.6 4.7 %fusion.9 = f32[1024]{0:T(1024)S(1)} fusion(f32[1024]{0:T(1024)S(1)} %bitcast.48, f32[2560]{0:T(1024)S(1)} %bitcast_divide_fusion.2, bf16[2560,1024]{0,1:T(8,128)(2,1)} %get-tuple-element.3, f32[2560]{0:T(1024)S(1)} %bitcast_divide_fusion.1), kind=kLoop, calls=%fused_computation.18 | loop fusion | flops 15727616 | bytes 5271552 | tf_op jit(solution)/shard_map/reduce_sum | solution.py:51
  176.3 14.3 %all_to_all.91 = f32[16,8,128]{2,1,0:T(8,128)S(1)} all-to-all(f32[16,8,128]{2,1,0:T(8,128)S(1)} %broadcast_in_dim.84), channel_id=1, replica_groups=mesh['y'=4,'zl'=8,'x'=4,'zh'=2,'c'=2] {'zh','zl'}, dimensions={0} | all-to-all | bytes 131072 | tf_op jit(solution)/shard_map/all_to_all | solution.py:14
  190.7 5.2 %fusion.4 = f32[2560]{0:T(1024)S(1)} fusion(bf16[2560,1024]{0,1:T(8,128)(2,1)} %get-tuple-element.3, f32[1024]{0:T(1024)S(1)} %bitcast.52, f32[1024]{0:T(1024)S(1)} %bitcast.49, f32[2560]{0:T(1024)S(1)} %bitcast_divide_fusion.2, f32[2560]{0:T(1024)S(1)} %bitcast_divide_fusion.1), kind=kLoop, calls=%fused_computation.12 | loop fusion | flops 20968960 | bytes 5281792 | tf_op jit(solution)/shard_map/reduce_sum | solution.py:53
  196.0 15.4 %all_to_all.92 = f32[32,20,128]{2,1,0:T(8,128)S(1)} all-to-all(f32[32,20,128]{2,1,0:T(8,128)S(1)} %broadcast_in_dim.86), channel_id=1, replica_groups=mesh['y'=4,'zl'=8,'x'=4,'zh'=2,'c'=2] {'y','x','c'}, dimensions={0} | all-to-all | bytes 655360 | tf_op jit(solution)/shard_map/all_to_all | solution.py:14
  211.4 5.4 %fusion.8 = f32[1024]{0:T(1024)S(1)} fusion(bf16[2560,1024]{0,1:T(8,128)(2,1)} %get-tuple-element.3, f32[2560]{0:T(1024)S(1)} %bitcast_divide_fusion, f32[1024]{0:T(1024)S(1)} %bitcast.53, f32[1024]{0:T(1024)S(1)} %bitcast.50, f32[2560]{0:T(1024)S(1)} %bitcast_divide_fusion.2, f32[2560]{0:T(1024)S(1)} %bitcast_divide_fusion.1), kind=kLoop, calls=%fused_computation.16 | loop fusion | flops 23591936 | bytes 5285888 | tf_op jit(solution)/shard_map/reduce_sum | solution.py:51
  216.8 0.6 broadcast_in_dim.88
  217.4 4.0 %all-to-all-start.9 = ((f32[16,8,128]{2,1,0:T(8,128)}), f32[16,8,128]{2,1,0:T(8,128)S(1)}, u32[]{:S(2)}, u32[]{:S(2)}) async-start(f32[16,8,128]{2,1,0:T(8,128)} %broadcast_in_dim.88), calls=%async_computation.9 | async-start | bytes 131072 | tf_op jit(solution)/shard_map/all_to_all | solution.py:14
  221.4 11.2 %all-to-all-done.9 = f32[16,8,128]{2,1,0:T(8,128)S(1)} async-done(((f32[16,8,128]{2,1,0:T(8,128)}), f32[16,8,128]{2,1,0:T(8,128)S(1)}, u32[]{:S(2)}, u32[]{:S(2)}) %all-to-all-start.9) | async-done | bytes 65568 | tf_op jit(solution)/shard_map/all_to_all | solution.py:14
  232.6 0.1 dynamic-slice_bitcast_fusion
  232.7 0.6 broadcast_in_dim.90
  233.3 3.2 %all-to-all-start.10 = ((f32[4,4,128]{2,1,0:T(4,128)}), f32[4,4,128]{2,1,0:T(4,128)S(1)}, u32[]{:S(2)}, u32[]{:S(2)}) async-start(f32[4,4,128]{2,1,0:T(4,128)} %broadcast_in_dim.90), calls=%async_computation.10 | async-start | bytes 16384 | tf_op jit(solution)/shard_map/all_to_all | solution.py:14
  236.5 6.3 %fusion.6 = f32[2560]{0:T(1024)S(1)} fusion(bf16[2560,1024]{0,1:T(8,128)(2,1)} %get-tuple-element.3, f32[1024]{0:T(1024)S(1)} %bitcast.61, f32[2560]{0:T(1024)S(1)} %bitcast_divide_fusion, f32[1024]{0:T(1024)S(1)} %bitcast.54, f32[1024]{0:T(1024)S(1)} %bitcast.51, f32[2560]{0:T(1024)S(1)} %bitcast_divide_fusion.2, f32[2560]{0:T(1024)S(1)} %bitcast_divide_fusion.1), kind=kLoop, calls=%fused_computation.14 | loop fusion | flops 28833280 | bytes 5296128 | tf_op jit(solution)/shard_map/reduce_sum | solution.py:53
  242.8 0.0 all-to-all-done.10
  242.8 0.7 broadcast_in_dim.92
  243.5 9.6 %all-to-all-start.11 = ((f32[64,5,128]{2,1,0:T(8,128)}), f32[64,5,128]{2,1,0:T(8,128)S(1)}, u32[]{:S(2)}, u32[]{:S(2)}) async-start(f32[64,5,128]{2,1,0:T(8,128)} %bitcast.20), calls=%async_computation.11 | async-start | bytes 524288 | tf_op jit(solution)/shard_map/all_to_all | solution.py:14
  253.2 26.3 %all-to-all-done.11 = f32[64,5,128]{2,1,0:T(8,128)S(1)} async-done(((f32[64,5,128]{2,1,0:T(8,128)}), f32[64,5,128]{2,1,0:T(8,128)S(1)}, u32[]{:S(2)}, u32[]{:S(2)}) %all-to-all-start.11) | async-done | bytes 163872 | tf_op jit(solution)/shard_map/all_to_all | solution.py:14
  279.5 0.1 reshape.93
  279.6 0.7 reshape.94
  280.3 0.6 copy.37
  (19 shorter events, 0.4 us)
Async XLA Ops:
  0.6 51.6 %copy-start = (bf16[1024,128]{1,0:T(8,128)(2,1)S(1)}, bf16[1024,128]{1,0:T(8,128)(2,1)}, u32[]{:S(2)}) copy-start(bf16[1024,128]{1,0:T(8,128)(2,1)} %param.7) | copy-start | bytes 786436
  0.6 70.5 %copy-start.1 = (bf16[1024,128]{1,0:T(8,128)(2,1)S(1)}, bf16[1024,128]{1,0:T(8,128)(2,1)}, u32[]{:S(2)}) copy-start(bf16[1024,128]{1,0:T(8,128)(2,1)} %param.8) | copy-start | bytes 786436
  2.8 41.7 %all-to-all-start = ((bf16[16,80,64]{1,2,0:T(8,128)(2,1)}), bf16[16,80,64]{1,2,0:T(8,128)(2,1)S(1)}, u32[]{:S(2)}, u32[]{:S(2)}) async-start(bf16[16,80,64]{1,2,0:T(8,128)(2,1)} %copy.23), calls=%async_computation | async-start | bytes 524288 | tf_op jit(solution)/shard_map/all_to_all | solution.py:23
  44.5 19.5 %all-to-all-start.2 = ((bf16[32,2,1024]{2,1,0:T(2,128)(2,1)}), bf16[32,2,1024]{2,1,0:T(2,128)(2,1)S(1)}, u32[]{:S(2)}, u32[]{:S(2)}) async-start(bf16[32,2,1024]{2,1,0:T(2,128)(2,1)} %reshape.102), calls=%async_computation.2 | async-start | bytes 262144 | tf_op jit(solution)/shard_map/all_to_all | solution.py:25
  64.9 19.0 %all-to-all-start.1 = ((bf16[32,80,128]{2,1,0:T(8,128)(2,1)}), bf16[32,80,128]{2,1,0:T(8,128)(2,1)S(1)}, u32[]{:S(2)}, u32[]{:S(2)}) async-start(bf16[32,80,128]{2,1,0:T(8,128)(2,1)} %broadcast_in_dim.74), calls=%async_computation.1 | async-start | bytes 1310720 | tf_op jit(solution)/shard_map/all_to_all | solution.py:14
  84.6 23.0 %all-to-all-start.3 = ((bf16[16,64,128]{2,1,0:T(8,128)(2,1)}), bf16[16,64,128]{2,1,0:T(8,128)(2,1)S(1)}, u32[]{:S(2)}, u32[]{:S(2)}) async-start(bf16[16,64,128]{2,1,0:T(8,128)(2,1)} %broadcast_in_dim.75), calls=%async_computation.3 | async-start | bytes 524288 | tf_op jit(solution)/shard_map/all_to_all | solution.py:14
  217.4 15.1 %all-to-all-start.9 = ((f32[16,8,128]{2,1,0:T(8,128)}), f32[16,8,128]{2,1,0:T(8,128)S(1)}, u32[]{:S(2)}, u32[]{:S(2)}) async-start(f32[16,8,128]{2,1,0:T(8,128)} %broadcast_in_dim.88), calls=%async_computation.9 | async-start | bytes 131072 | tf_op jit(solution)/shard_map/all_to_all | solution.py:14
  233.3 9.5 %all-to-all-start.10 = ((f32[4,4,128]{2,1,0:T(4,128)}), f32[4,4,128]{2,1,0:T(4,128)S(1)}, u32[]{:S(2)}, u32[]{:S(2)}) async-start(f32[4,4,128]{2,1,0:T(4,128)} %broadcast_in_dim.90), calls=%async_computation.10 | async-start | bytes 16384 | tf_op jit(solution)/shard_map/all_to_all | solution.py:14
  243.5 35.9 %all-to-all-start.11 = ((f32[64,5,128]{2,1,0:T(8,128)}), f32[64,5,128]{2,1,0:T(8,128)S(1)}, u32[]{:S(2)}, u32[]{:S(2)}) async-start(f32[64,5,128]{2,1,0:T(8,128)} %bitcast.20), calls=%async_computation.11 | async-start | bytes 524288 | tf_op jit(solution)/shard_map/all_to_all | solution.py:14

commit v2 on v1

v2 whole, which is shorter than its diff:
```python
import functools

import jax
import jax.numpy as jnp
from jax import lax
from jax.experimental import pallas as pl
from jax.experimental.pallas import tpu as pltpu
from jax.sharding import Mesh, PartitionSpec as P

ITERS = 3
FINE = (("y", 4), ("zl", 8), ("x", 4), ("zh", 2), ("c", 2))
PLANE = ("y", "x", "c")
RING = ("zh", "zl")
E = 128
NBUY = 2560
NGOOD = 1024
LB = NBUY // 128
GT = NGOOD // 128


def softplus(x):
    return jnp.maximum(x, 0.0) + jnp.log1p(jnp.exp(-jnp.abs(x)))


def values_kernel(goods_ref, buyers_ref, money_ref, values_ref, out_ref, total, rows):
    step = pl.program_id(0)

    @pl.when(step == 0)
    def _():
        total[...] = jnp.zeros_like(total)

    for b in range(NBUY // 256):
        cols = slice(256 * b, 256 * b + 256)
        scores = lax.dot_general(
            goods_ref[...], buyers_ref[cols, :], (((1,), (1,)), ((), ())), preferred_element_type=jnp.float32
        )
        rounded = softplus(scores * E ** (-0.5)).astype(jnp.bfloat16)
        values_ref[:, cols] = rounded
        total[:, cols] += jnp.sum(rounded.astype(jnp.float32).reshape(-1, 8, 256), 0)

    @pl.when(step == pl.num_programs(0) - 1)
    def _():
        whole = jnp.sum(total[...], 0, keepdims=True)
        for b in range(LB):
            rows[b : b + 1, :] = whole[:, 128 * b : 128 * b + 128]
        rows[LB : LB + 1, :] = money_ref[...]
        for p in range(out_ref.shape[0]):
            out_ref[p] = rows[0 : LB + 1, :]


def powered(v, k):
    square = v * v if k >= 2 else None
    return {1: lambda: v, 2: lambda: square, 3: lambda: square * v, 4: lambda: square * square}[k]()


def fetch(values_hbm, values, sems):
    copies = [
        pltpu.make_async_copy(values_hbm.at[pl.ds(128 * q, 128)], values.at[pl.ds(128 * q, 128)], sems.at[q])
        for q in range(GT)
    ]
    for copy in copies:
        copy.start()
    return copies


def price_kernel(k, got_ref, money_ref, values_hbm, out_ref, values, scale, sums, sems):
    copies = fetch(values_hbm, values, sems)
    total = got_ref[0, 0:LB, :]
    for p in range(1, got_ref.shape[0]):
        total = total + got_ref[p, 0:LB, :]
    scale[...] = money_ref[...] / total
    for q in range(GT):
        copies[q].wait()

        def chunk(i, _, q=q):
            at = pl.multiple_of(128 * q + 16 * i, 16)
            acc = None
            for b in range(LB):
                v = values[pl.ds(at, 16), 128 * b : 128 * b + 128].astype(jnp.float32)
                term = powered(v, k) * scale[b : b + 1, :]
                acc = term if acc is None else acc + term
            sums[pl.ds(pl.multiple_of(16 * i, 16), 16), :] = acc
            return 0

        lax.fori_loop(0, 8, chunk, 0, unroll=2)
        row = jnp.sum(sums[...].T, 0, keepdims=True)
        for p in range(out_ref.shape[0]):
            out_ref[p, q : q + 1, :] = row


def utility_kernel(k, got_ref, *refs):
    last = k == ITERS
    if last:
        before_ref, zh_ref, values_hbm, out_ref, values, inverse, spare, sems = refs
    else:
        values_hbm, out_ref, sum_ref, values, inverse, spare, sems = refs
    copies = fetch(values_hbm, values, sems)
    total = got_ref[0]
    for p in range(1, got_ref.shape[0]):
        total = total + got_ref[p]
    inverse[...] = 1.0 / total
    if last:
        spare[0:8, :] = total / before_ref[...]
        half = spare[pl.ds(pl.multiple_of(4 * zh_ref[0], 4), 4), :]
        for p in range(out_ref.shape[0]):
            out_ref[p, LB : LB + 4, :] = half
    else:
        sum_ref[...] = total
    accs = tuple(jnp.zeros((8, 128), jnp.float32) for _ in range(LB))
    for q in range(GT):
        copies[q].wait()
        spare[...] = jnp.broadcast_to(inverse[q : q + 1, :], (128, 128)).T

        def chunk(i, accs, q=q):
            at = pl.multiple_of(128 * q + 16 * i, 16)
            c = spare[pl.ds(pl.multiple_of(16 * i, 16), 16), :]
            new = []
            for b in range(LB):
                v = values[pl.ds(at, 16), 128 * b : 128 * b + 128].astype(jnp.float32)
                term = powered(v, k + 1) * c
                new.append(accs[b] + (term[0:8] + term[8:16]))
            return tuple(new)

        accs = lax.fori_loop(0, 8, chunk, accs)
    for b in range(LB):
        spare[b : b + 1, :] = jnp.sum(accs[b], 0, keepdims=True)
    for p in range(out_ref.shape[0]):
        out_ref[p, 0:LB, :] = spare[0:LB, :]


VM = pl.BlockSpec(memory_space=pltpu.VMEM)
PARAMS = pltpu.CompilerParams(vmem_limit_bytes=16 << 20)


def values_call(goods_emb, buyer_emb, money_row):
    return pl.pallas_call(
        values_kernel,
        grid=(GT,),
        in_specs=[
            pl.BlockSpec((128, E), lambda i: (i, 0)),
            pl.BlockSpec((NBUY, E), lambda i: (0, 0)),
            pl.BlockSpec((1, 128), lambda i: (0, 0)),
        ],
        out_specs=[
            pl.BlockSpec((128, NBUY), lambda i: (i, 0)),
            pl.BlockSpec((32, LB + 1, 128), lambda i: (0, 0, 0)),
        ],
        out_shape=[
            jax.ShapeDtypeStruct((NGOOD, NBUY), jnp.bfloat16),
            jax.ShapeDtypeStruct((32, LB + 1, 128), jnp.float32),
        ],
        scratch_shapes=[pltpu.VMEM((8, NBUY), jnp.float32), pltpu.VMEM((24, 128), jnp.float32)],
        compiler_params=PARAMS,
    )(goods_emb, buyer_emb, money_row)


def held():
    return pltpu.VMEM((NGOOD, NBUY), jnp.bfloat16)


def price_call(k, got, money, values):
    return pl.pallas_call(
        functools.partial(price_kernel, k),
        in_specs=[VM, VM, pl.BlockSpec(memory_space=pl.ANY)],
        out_specs=VM,
        out_shape=jax.ShapeDtypeStruct((16, GT, 128), jnp.float32),
        scratch_shapes=[
            held(),
            pltpu.VMEM((LB, 128), jnp.float32),
            pltpu.VMEM((128, 128), jnp.float32),
            pltpu.SemaphoreType.DMA((GT,)),
        ],
        compiler_params=PARAMS,
    )(got, money, values)


def utility_call(k, got, values, before=None, zh=None):
    last = k == ITERS
    scratch = [held(), pltpu.VMEM((GT, 128), jnp.float32), pltpu.VMEM((128, 128), jnp.float32), pltpu.SemaphoreType.DMA((GT,))]
    if last:
        return pl.pallas_call(
            functools.partial(utility_kernel, k),
            in_specs=[VM, VM, pl.BlockSpec(memory_space=pltpu.SMEM), pl.BlockSpec(memory_space=pl.ANY)],
            out_specs=VM,
            out_shape=jax.ShapeDtypeStruct((32, LB + 4, 128), jnp.float32),
            scratch_shapes=scratch,
            compiler_params=PARAMS,
        )(got, before, zh, values)
    return pl.pallas_call(
        functools.partial(utility_kernel, k),
        in_specs=[VM, pl.BlockSpec(memory_space=pl.ANY)],
        out_specs=[VM, VM],
        out_shape=[jax.ShapeDtypeStruct((32, LB, 128), jnp.float32), jax.ShapeDtypeStruct((GT, 128), jnp.float32)],
        scratch_shapes=scratch,
        compiler_params=PARAMS,
    )(got, values)


def exchange(x, axes):
    return lax.all_to_all(x, axes, 0, 0, tiled=True)


def spread_out(x, axes, n):
    return exchange(jnp.broadcast_to(x[None], (n,) + x.shape), axes)


def per_device(buyer_hidden, goods_hidden, buyer_proj, goods_proj, endowment):
    x, y, zh, c = (lax.axis_index(a) for a in ("x", "y", "zh", "c"))
    rows = lax.all_to_all(buyer_hidden, ("x", "zh", "c"), 0, 1, tiled=True)
    buyer_own = jnp.dot(rows, buyer_proj, preferred_element_type=jnp.float32).astype(jnp.bfloat16)
    rows = lax.all_to_all(goods_hidden, ("y", "zl"), 0, 1, tiled=True)
    goods_own = jnp.dot(rows, goods_proj, preferred_element_type=jnp.float32).astype(jnp.bfloat16)
    buyer_emb = spread_out(buyer_own, PLANE, 32).reshape(-1, E)
    goods_emb = spread_out(goods_own, RING, 16).reshape(-1, E)

    mine = lax.dynamic_index_in_dim(endowment.reshape(4, 2, 160), zh, 1, keepdims=False).reshape(5, 128)
    money_row = lax.dynamic_slice(mine, (jnp.minimum(x * 2 + c, 4), 0), (1, 128))

    values, sent = values_call(goods_emb, buyer_emb, money_row)
    got = exchange(sent, PLANE)
    money = got[:, LB].reshape(4, 8, 128)[:, :5].reshape(LB, 128)
    for k in range(1, ITERS):
        ring = exchange(price_call(k, got, money, values), RING)
        sent, before = utility_call(k, ring, values)
        got = exchange(sent, PLANE)
    ring = exchange(price_call(ITERS, got, money, values), RING)
    final = exchange(utility_call(ITERS, ring, values, before, zh.reshape(1).astype(jnp.int32)), PLANE)
    prices = lax.dynamic_index_in_dim(final.reshape(4, 8, LB + 4, 128), x * 2 + c, 1, keepdims=False)[:, LB:].reshape(-1)
    five = lambda a, axis: lax.dynamic_slice_in_dim(a, 5 * y, 5, axis)
    mine_total = jnp.sum(five(final, 1), 0) * five(money, 0) / jnp.sum(five(got, 1), 0)
    other = lax.ppermute(mine_total, "zh", [(0, 1), (1, 0)])
    first = jnp.where(zh == 0, mine_total, other).reshape(4, 160)
    second = jnp.where(zh == 0, other, mine_total).reshape(4, 160)
    utility = jnp.stack([first, second], 1).reshape(-1)
    return (prices, utility)


def solution(mesh):
    fine = Mesh(mesh.devices.reshape([n for _, n in FINE]), [a for a, _ in FINE])
    buyers, goods = ("y", "zl"), ("x", "zh", "c")
    placed = (P(buyers, goods), P(goods, buyers), P(), P(), P(buyers))
    return jax.shard_map(
        per_device, mesh=fine, in_specs=placed, out_specs=(P(goods), P(buyers)), check_vma=False
    )
```

time: 282 us -> 272 us (0.965)
  the two profiles are of different devices: /device:TPU:33 before, /device:TPU:1 now
where the time goes in v2:
time: 272 us
  blocking collectives  95.4 us (35%)
  waiting for transfers between devices  71.2 us (26%)
  starting transfers between devices  54 us (20%)
  Pallas kernels  36.8 us (14%)
  local copies, waits for them, and re-layouts  12.6 us (5%)
    all_to_all x6, blocking collectives, exchange(): return lax.all_to_all(x, axes, 0, 0, tiled=True)  95.4 us
    all_to_all x3, waiting for transfers between devices, exchange(): return lax.all_to_all(x, axes, 0, 0, tiled=True)  36.3 us
    all_to_all x1, starting transfers between devices, per_device(): rows = lax.all_to_all(buyer_hidden, ('x', 'zh', 'c'), 0, 1, tiled=True)  19.1 us
    all_to_all x3, starting transfers between devices, exchange(): return lax.all_to_all(x, axes, 0, 0, tiled=True)  16.4 us
    all_to_all x1, starting transfers between devices, per_device(): rows = lax.all_to_all(goods_hidden, ('y', 'zl'), 0, 1, tiled=True)  15.3 us
    all_to_all x1, waiting for transfers between devices, per_device(): rows = lax.all_to_all(buyer_hidden, ('x', 'zh', 'c'), 0, 1, tiled=True)  14.2 us
    pallas_call x3, Pallas kernels, price_call(): pl.pallas_call(functools.partial(price_kernel, k), in_specs=[VM, VM, pl.B...  13.2 us
    all_to_all x1, waiting for transfers between devices, per_device(): rows = lax.all_to_all(goods_hidden, ('y', 'zl'), 0, 1, tiled=True)  11.5 us
  transfers between devices with their start and end apart: 6, of which 6 were waited for; matrix products, arithmetic and copies ran while one was open for 1% of the time, Pallas kernels for 0%

profile of v2, /device:TPU:1, one launch (start us, length us, event | category | flops | bytes accessed | tf_op | source)
XLA Modules:
  0.0 271.5 jit_solution(12950641929247794994)
XLA Ops:
  0.6 0.0 copy-start
  0.6 0.0 copy-start.3
  0.7 0.0 copy-start.4
  0.7 1.4 all_to_all.60
  2.0 0.8 copy.16
  2.8 19.1 %all-to-all-start.2 = ((bf16[16,80,64]{1,2,0:T(8,128)(2,1)}), bf16[16,80,64]{1,2,0:T(8,128)(2,1)S(1)}, u32[]{:S(2)}, u32[]{:S(2)}) async-start(bf16[16,80,64]{1,2,0:T(8,128)(2,1)} %copy.16), calls=%async_computation.2 | async-start | bytes 524288 | tf_op jit(solution)/shard_map/all_to_all | solution.py:209
  21.9 1.2 all_to_all.55
  23.0 0.1 copy.22
  23.1 0.8 reshape.50
  24.0 14.2 %all-to-all-done.2 = bf16[16,80,64]{1,2,0:T(8,128)(2,1)S(1)} async-done(((bf16[16,80,64]{1,2,0:T(8,128)(2,1)}), bf16[16,80,64]{1,2,0:T(8,128)(2,1)S(1)}, u32[]{:S(2)}, u32[]{:S(2)}) %all-to-all-start.2) | async-done | bytes 163872 | tf_op jit(solution)/shard_map/all_to_all | solution.py:209
  38.2 15.3 %all-to-all-start = ((bf16[32,2,1024]{2,1,0:T(2,128)(2,1)}), bf16[32,2,1024]{2,1,0:T(2,128)(2,1)S(1)}, u32[]{:S(2)}, u32[]{:S(2)}) async-start(bf16[32,2,1024]{2,1,0:T(2,128)(2,1)} %reshape.50), calls=%async_computation | async-start | bytes 262144 | tf_op jit(solution)/shard_map/all_to_all | solution.py:211
  53.5 0.0 copy-done
  53.5 0.2 convolution_convert_fusion
  53.8 11.5 %all-to-all-done = bf16[32,2,1024]{2,1,0:T(2,128)(2,1)S(1)} async-done(((bf16[32,2,1024]{2,1,0:T(2,128)(2,1)}), bf16[32,2,1024]{2,1,0:T(2,128)(2,1)S(1)}, u32[]{:S(2)}, u32[]{:S(2)}) %all-to-all-start) | async-done | bytes 131104 | tf_op jit(solution)/shard_map/all_to_all | solution.py:211
  65.3 0.9 broadcast_in_dim.5
  66.2 7.2 %all-to-all-start.3 = ((bf16[32,80,128]{2,1,0:T(8,128)(2,1)}), bf16[32,80,128]{2,1,0:T(8,128)(2,1)S(1)}, u32[]{:S(2)}, u32[]{:S(2)}) async-start(bf16[32,80,128]{2,1,0:T(8,128)(2,1)} %broadcast_in_dim.5), calls=%async_computation.3 | async-start | bytes 1310720 | tf_op jit(solution)/shard_map/all_to_all | solution.py:200
  73.4 0.2 reshape.51
  73.6 0.0 copy-done.3
  73.6 0.2 convolution_convert_fusion.1
  73.9 12.5 %all-to-all-done.3 = bf16[32,80,128]{2,1,0:T(8,128)(2,1)S(1)} async-done(((bf16[32,80,128]{2,1,0:T(8,128)(2,1)}), bf16[32,80,128]{2,1,0:T(8,128)(2,1)S(1)}, u32[]{:S(2)}, u32[]{:S(2)}) %all-to-all-start.3) | async-done | bytes 655392 | tf_op jit(solution)/shard_map/all_to_all | solution.py:200
  86.3 0.8 broadcast_in_dim.4
  87.1 3.6 %all-to-all-start.1 = ((bf16[16,64,128]{2,1,0:T(8,128)(2,1)}), bf16[16,64,128]{2,1,0:T(8,128)(2,1)S(1)}, u32[]{:S(2)}, u32[]{:S(2)}) async-start(bf16[16,64,128]{2,1,0:T(8,128)(2,1)} %broadcast_in_dim.4), calls=%async_computation.1 | async-start | bytes 524288 | tf_op jit(solution)/shard_map/all_to_all | solution.py:200
  90.7 0.0 copy-done.4
  90.7 0.1 reshape.42
  90.8 0.1 reshape.43
  90.9 13.6 %all-to-all-done.1 = bf16[16,64,128]{2,1,0:T(8,128)(2,1)S(1)} async-done(((bf16[16,64,128]{2,1,0:T(8,128)(2,1)}), bf16[16,64,128]{2,1,0:T(8,128)(2,1)S(1)}, u32[]{:S(2)}, u32[]{:S(2)}) %all-to-all-start.1) | async-done | bytes 262176 | tf_op jit(solution)/shard_map/all_to_all | solution.py:200
  104.5 8.1 %shard_map.68 = (bf16[1024,2560]{1,0:T(8,128)(2,1)S(1)}, f32[32,21,128]{2,1,0:T(8,128)S(1)}) custom-call(bf16[1024,128]{1,0:T(8,128)(2,1)S(1)} %bitcast.28, bf16[2560,128]{1,0:T(8,128)(2,1)S(1)} %bitcast.27, f32[1,128]{1,0:T(1,128)S(1)} %constant_dynamic-slice_fusion.money_ref), custom_call_target="tpu_custom_call" | custom-call | tf_op jit(solution)/shard_map/pallas_call | solution.py:136
  112.6 0.0 copy-start.1
  112.6 2.3 copy-done.1
  114.9 18.8 %all_to_all.83.got_ref = f32[32,21,128]{2,1,0:T(8,128)S(1)} all-to-all(f32[32,21,128]{2,1,0:T(8,128)S(1)} %get-tuple-element.7), channel_id=1, replica_groups=mesh['y'=4,'zl'=8,'x'=4,'zh'=2,'c'=2] {'y','x','c'}, dimensions={0} | all-to-all | bytes 688128 | tf_op jit(solution)/shard_map/all_to_all | solution.py:200
  133.8 0.0 copy-start.2
  133.8 2.5 copy-done.2
  136.3 4.1 %shard_map.69 = f32[16,8,128]{2,1,0:T(8,128)S(1)} custom-call(f32[32,21,128]{2,1,0:T(8,128)S(1)} %all_to_all.83.got_ref, f32[20,128]{1,0:T(8,128)S(1)} %reshape.44.money_ref, bf16[1024,2560]{1,0:T(8,128)(2,1)S(1)} %copy-done.2), custom_call_target="tpu_custom_call" | custom-call | tf_op jit(solution)/shard_map/pallas_call | solution.py:162
  140.4 17.1 %all_to_all.84.got_ref = f32[16,8,128]{2,1,0:T(8,128)S(1)} all-to-all(f32[16,8,128]{2,1,0:T(8,128)S(1)} %shard_map.69), channel_id=1, replica_groups=mesh['y'=4,'zl'=8,'x'=4,'zh'=2,'c'=2] {'zh','zl'}, dimensions={0} | all-to-all | bytes 131072 | tf_op jit(solution)/shard_map/all_to_all | solution.py:200
  157.5 5.0 %shard_map.70 = (f32[32,20,128]{2,1,0:T(8,128)S(1)}, f32[8,128]{1,0:T(8,128)}) custom-call(f32[16,8,128]{2,1,0:T(8,128)S(1)} %all_to_all.84.got_ref, bf16[1024,2560]{1,0:T(8,128)(2,1)S(1)} %copy-done.2), custom_call_target="tpu_custom_call" | custom-call | tf_op jit(solution)/shard_map/pallas_call | solution.py:189
  162.6 15.4 %all_to_all.85.got_ref = f32[32,20,128]{2,1,0:T(8,128)S(1)} all-to-all(f32[32,20,128]{2,1,0:T(8,128)S(1)} %get-tuple-element.9), channel_id=1, replica_groups=mesh['y'=4,'zl'=8,'x'=4,'zh'=2,'c'=2] {'y','x','c'}, dimensions={0} | all-to-all | bytes 655360 | tf_op jit(solution)/shard_map/all_to_all | solution.py:200
  178.0 4.4 %shard_map.71 = f32[16,8,128]{2,1,0:T(8,128)S(1)} custom-call(f32[32,20,128]{2,1,0:T(8,128)S(1)} %all_to_all.85.got_ref, f32[20,128]{1,0:T(8,128)S(1)} %reshape.44.money_ref, bf16[1024,2560]{1,0:T(8,128)(2,1)S(1)} %copy-done.2), custom_call_target="tpu_custom_call" | custom-call | tf_op jit(solution)/shard_map/pallas_call | solution.py:162
  182.4 14.3 %all_to_all.86.got_ref = f32[16,8,128]{2,1,0:T(8,128)S(1)} all-to-all(f32[16,8,128]{2,1,0:T(8,128)S(1)} %shard_map.71), channel_id=1, replica_groups=mesh['y'=4,'zl'=8,'x'=4,'zh'=2,'c'=2] {'zh','zl'}, dimensions={0} | all-to-all | bytes 131072 | tf_op jit(solution)/shard_map/all_to_all | solution.py:200
  196.7 4.8 %shard_map.72 = (f32[32,20,128]{2,1,0:T(8,128)S(1)}, f32[8,128]{1,0:T(8,128)S(1)}) custom-call(f32[16,8,128]{2,1,0:T(8,128)S(1)} %all_to_all.86.got_ref, bf16[1024,2560]{1,0:T(8,128)(2,1)S(1)} %copy-done.2), custom_call_target="tpu_custom_call" | custom-call | tf_op jit(solution)/shard_map/pallas_call | solution.py:189
  201.5 15.4 %all_to_all.87.got_ref = f32[32,20,128]{2,1,0:T(8,128)S(1)} all-to-all(f32[32,20,128]{2,1,0:T(8,128)S(1)} %get-tuple-element.10), channel_id=1, replica_groups=mesh['y'=4,'zl'=8,'x'=4,'zh'=2,'c'=2] {'y','x','c'}, dimensions={0} | all-to-all | bytes 655360 | tf_op jit(solution)/shard_map/all_to_all | solution.py:200
  217.0 4.7 %shard_map.73 = f32[16,8,128]{2,1,0:T(8,128)S(1)} custom-call(f32[32,20,128]{2,1,0:T(8,128)S(1)} %all_to_all.87.got_ref, f32[20,128]{1,0:T(8,128)S(1)} %reshape.44.money_ref, bf16[1024,2560]{1,0:T(8,128)(2,1)S(1)} %copy-done.2), custom_call_target="tpu_custom_call" | custom-call | tf_op jit(solution)/shard_map/pallas_call | solution.py:162
  221.7 14.3 %all_to_all.88.got_ref = f32[16,8,128]{2,1,0:T(8,128)S(1)} all-to-all(f32[16,8,128]{2,1,0:T(8,128)S(1)} %shard_map.73), channel_id=1, replica_groups=mesh['y'=4,'zl'=8,'x'=4,'zh'=2,'c'=2] {'zh','zl'}, dimensions={0} | all-to-all | bytes 131072 | tf_op jit(solution)/shard_map/all_to_all | solution.py:200
  236.0 5.6 %shard_map.74 = f32[32,24,128]{2,1,0:T(8,128)} custom-call(f32[16,8,128]{2,1,0:T(8,128)S(1)} %all_to_all.88.got_ref, f32[8,128]{1,0:T(8,128)S(1)} %get-tuple-element.11.refs_0_, s32[1]{0:T(128)} %bitcast.7.refs_1_, bf16[1024,2560]{1,0:T(8,128)(2,1)S(1)} %copy-done.2), custom_call_target="tpu_custom_call" | custom-call | tf_op jit(solution)/shard_map/pallas_call | solution.py:181
  241.6 5.7 %all-to-all-start.10 = ((f32[32,24,128]{2,1,0:T(8,128)}), f32[32,24,128]{2,1,0:T(8,128)S(1)}, u32[]{:S(2)}, u32[]{:S(2)}) async-start(f32[32,24,128]{2,1,0:T(8,128)} %shard_map.74), calls=%async_computation.10 | async-start | bytes 786432 | tf_op jit(solution)/shard_map/all_to_all | solution.py:200
  247.3 10.2 %all-to-all-done.10 = f32[32,24,128]{2,1,0:T(8,128)S(1)} async-done(((f32[32,24,128]{2,1,0:T(8,128)}), f32[32,24,128]{2,1,0:T(8,128)S(1)}, u32[]{:S(2)}, u32[]{:S(2)}) %all-to-all-start.10) | async-done | bytes 393248 | tf_op jit(solution)/shard_map/all_to_all | solution.py:200
  257.6 3.2 %collective-permute-start = (f32[5,128]{1,0:T(8,128)S(1)}, f32[5,128]{1,0:T(8,128)S(1)}, u32[]{:S(2)}, u32[]{:S(2)}) collective-permute-start(f32[5,128]{1,0:T(8,128)S(1)} %multiply_divide_fusion), channel_id=1, source_target_pairs={{0,2},{2,0},{1,3},{3,1},{4,6},{6,4},{5,7},{7,5},{8,10},{10,8},{9,1... | collective-permute-start | bytes 7688 | tf_op jit(solution)/shard_map/ppermute | solution.py:231
  260.8 0.6 slice.14
  261.4 9.2 %collective-permute-done = f32[5,128]{1,0:T(8,128)S(1)} collective-permute-done((f32[5,128]{1,0:T(8,128)S(1)}, f32[5,128]{1,0:T(8,128)S(1)}, u32[]{:S(2)}, u32[]{:S(2)}) %collective-permute-start) | collective-permute-done | bytes 2592 | tf_op jit(solution)/shard_map/ppermute | solution.py:231
  270.7 0.1 stack_reshape.8
  270.8 0.1 stack_reshape.9
  270.9 0.7 reshape.48
  (10 shorter events, 0.2 us)
Async XLA Ops:
  0.6 52.9 %copy-start = (bf16[1024,128]{1,0:T(8,128)(2,1)S(1)}, bf16[1024,128]{1,0:T(8,128)(2,1)}, u32[]{:S(2)}) copy-start(bf16[1024,128]{1,0:T(8,128)(2,1)} %param.7) | copy-start | bytes 786436
  0.6 73.0 %copy-start.3 = (bf16[1024,128]{1,0:T(8,128)(2,1)S(1)}, bf16[1024,128]{1,0:T(8,128)(2,1)}, u32[]{:S(2)}) copy-start(bf16[1024,128]{1,0:T(8,128)(2,1)} %param.8) | copy-start | bytes 786436
  0.7 90.1 %copy-start.4 = (f32[1280]{0:T(1024)S(1)}, f32[1280]{0:T(1024)}, u32[]{:S(2)}) copy-start(f32[1280]{0:T(1024)} %param.9) | copy-start | bytes 15364
  2.8 35.4 %all-to-all-start.2 = ((bf16[16,80,64]{1,2,0:T(8,128)(2,1)}), bf16[16,80,64]{1,2,0:T(8,128)(2,1)S(1)}, u32[]{:S(2)}, u32[]{:S(2)}) async-start(bf16[16,80,64]{1,2,0:T(8,128)(2,1)} %copy.16), calls=%async_computation.2 | async-start | bytes 524288 | tf_op jit(solution)/shard_map/all_to_all | solution.py:209
  38.2 27.1 %all-to-all-start = ((bf16[32,2,1024]{2,1,0:T(2,128)(2,1)}), bf16[32,2,1024]{2,1,0:T(2,128)(2,1)S(1)}, u32[]{:S(2)}, u32[]{:S(2)}) async-start(bf16[32,2,1024]{2,1,0:T(2,128)(2,1)} %reshape.50), calls=%async_computation | async-start | bytes 262144 | tf_op jit(solution)/shard_map/all_to_all | solution.py:211
  66.2 20.1 %all-to-all-start.3 = ((bf16[32,80,128]{2,1,0:T(8,128)(2,1)}), bf16[32,80,128]{2,1,0:T(8,128)(2,1)S(1)}, u32[]{:S(2)}, u32[]{:S(2)}) async-start(bf16[32,80,128]{2,1,0:T(8,128)(2,1)} %broadcast_in_dim.5), calls=%async_computation.3 | async-start | bytes 1310720 | tf_op jit(solution)/shard_map/all_to_all | solution.py:200
  87.1 17.4 %all-to-all-start.1 = ((bf16[16,64,128]{2,1,0:T(8,128)(2,1)}), bf16[16,64,128]{2,1,0:T(8,128)(2,1)S(1)}, u32[]{:S(2)}, u32[]{:S(2)}) async-start(bf16[16,64,128]{2,1,0:T(8,128)(2,1)} %broadcast_in_dim.4), calls=%async_computation.1 | async-start | bytes 524288 | tf_op jit(solution)/shard_map/all_to_all | solution.py:200
  112.6 2.3 copy-start.1
  133.8 2.5 copy-start.2
  241.6 15.9 %all-to-all-start.10 = ((f32[32,24,128]{2,1,0:T(8,128)}), f32[32,24,128]{2,1,0:T(8,128)S(1)}, u32[]{:S(2)}, u32[]{:S(2)}) async-start(f32[32,24,128]{2,1,0:T(8,128)} %shard_map.74), calls=%async_computation.10 | async-start | bytes 786432 | tf_op jit(solution)/shard_map/all_to_all | solution.py:200
  257.6 13.1 %collective-permute-start = (f32[5,128]{1,0:T(8,128)S(1)}, f32[5,128]{1,0:T(8,128)S(1)}, u32[]{:S(2)}, u32[]{:S(2)}) collective-permute-start(f32[5,128]{1,0:T(8,128)S(1)} %multiply_divide_fusion), channel_id=1, source_target_pairs={{0,2},{2,0},{1,3},{3,1},{4,6},{6,4},{5,7},{7,5},{8,10},{10,8},{9,1... | collective-permute-start | bytes 7688 | tf_op jit(solution)/shard_map/ppermute | solution.py:231

commit v3 on v2

--- a/solution.py
+++ b/solution.py
@@ -53,24 +53,12 @@
     return {1: lambda: v, 2: lambda: square, 3: lambda: square * v, 4: lambda: square * square}[k]()
 
 
-def fetch(values_hbm, values, sems):
-    copies = [
-        pltpu.make_async_copy(values_hbm.at[pl.ds(128 * q, 128)], values.at[pl.ds(128 * q, 128)], sems.at[q])
-        for q in range(GT)
-    ]
-    for copy in copies:
-        copy.start()
-    return copies
-
-
-def price_kernel(k, got_ref, money_ref, values_hbm, out_ref, values, scale, sums, sems):
-    copies = fetch(values_hbm, values, sems)
+def price_kernel(k, got_ref, money_ref, values, out_ref, scale, sums):
     total = got_ref[0, 0:LB, :]
     for p in range(1, got_ref.shape[0]):
         total = total + got_ref[p, 0:LB, :]
     scale[...] = money_ref[...] / total
     for q in range(GT):
-        copies[q].wait()
 
         def chunk(i, _, q=q):
             at = pl.multiple_of(128 * q + 16 * i, 16)
@@ -91,10 +79,9 @@
 def utility_kernel(k, got_ref, *refs):
     last = k == ITERS
     if last:
-        before_ref, zh_ref, values_hbm, out_ref, values, inverse, spare, sems = refs
+        before_ref, zh_ref, values, out_ref, inverse, spare = refs
     else:
-        values_hbm, out_ref, sum_ref, values, inverse, spare, sems = refs
-    copies = fetch(values_hbm, values, sems)
+        values, out_ref, sum_ref, inverse, spare = refs
     total = got_ref[0]
     for p in range(1, got_ref.shape[0]):
         total = total + got_ref[p]
@@ -108,7 +95,6 @@
         sum_ref[...] = total
     accs = tuple(jnp.zeros((8, 128), jnp.float32) for _ in range(LB))
     for q in range(GT):
-        copies[q].wait()
         spare[...] = jnp.broadcast_to(inverse[q : q + 1, :], (128, 128)).T
 
         def chunk(i, accs, q=q):
@@ -150,25 +136,19 @@
             jax.ShapeDtypeStruct((32, LB + 1, 128), jnp.float32),
         ],
         scratch_shapes=[pltpu.VMEM((8, NBUY), jnp.float32), pltpu.VMEM((24, 128), jnp.float32)],
-        compiler_params=PARAMS,
+        compiler_params=pltpu.CompilerParams(vmem_limit_bytes=61 << 20),
     )(goods_emb, buyer_emb, money_row)
 
 
-def held():
-    return pltpu.VMEM((NGOOD, NBUY), jnp.bfloat16)
-
-
 def price_call(k, got, money, values):
     return pl.pallas_call(
         functools.partial(price_kernel, k),
-        in_specs=[VM, VM, pl.BlockSpec(memory_space=pl.ANY)],
+        in_specs=[VM, VM, VM],
         out_specs=VM,
         out_shape=jax.ShapeDtypeStruct((16, GT, 128), jnp.float32),
         scratch_shapes=[
-            held(),
             pltpu.VMEM((LB, 128), jnp.float32),
             pltpu.VMEM((128, 128), jnp.float32),
-            pltpu.SemaphoreType.DMA((GT,)),
         ],
         compiler_params=PARAMS,
     )(got, money, values)
@@ -176,11 +156,11 @@
 
 def utility_call(k, got, values, before=None, zh=None):
     last = k == ITERS
-    scratch = [held(), pltpu.VMEM((GT, 128), jnp.float32), pltpu.VMEM((128, 128), jnp.float32), pltpu.SemaphoreType.DMA((GT,))]
+    scratch = [pltpu.VMEM((GT, 128), jnp.float32), pltpu.VMEM((128, 128), jnp.float32)]
     if last:
         return pl.pallas_call(
             functools.partial(utility_kernel, k),
-            in_specs=[VM, VM, pl.BlockSpec(memory_space=pltpu.SMEM), pl.BlockSpec(memory_space=pl.ANY)],
+            in_specs=[VM, VM, pl.BlockSpec(memory_space=pltpu.SMEM), VM],
             out_specs=VM,
             out_shape=jax.ShapeDtypeStruct((32, LB + 4, 128), jnp.float32),
             scratch_shapes=scratch,
@@ -188,7 +168,7 @@
         )(got, before, zh, values)
     return pl.pallas_call(
         functools.partial(utility_kernel, k),
-        in_specs=[VM, pl.BlockSpec(memory_space=pl.ANY)],
+        in_specs=[VM, VM],
         out_specs=[VM, VM],
         out_shape=[jax.ShapeDtypeStruct((32, LB, 128), jnp.float32), jax.ShapeDtypeStruct((GT, 128), jnp.float32)],
         scratch_shapes=scratch,
@@ -196,22 +176,85 @@
     )(got, values)
 
 
+def pack_kernel(hidden_ref, out_ref):
+    rows = hidden_ref[...].T
+    for q in range(8):
+        at = 80 * (4 * (q // 2) + q % 2)
+        out_ref[q] = jnp.concatenate([rows[at : at + 80], rows[at + 160 : at + 240]], 1)
+
+
+def half_kernel(zh_ref, got_ref, proj_ref, mine_ref, other_ref, weights, both):
+    weights[...] = jnp.zeros_like(weights)
+    total = jnp.zeros((80, 2 * E), jnp.float32)
+    for q in range(8):
+        weights[q, 0:64, 0:E] = proj_ref[q]
+        weights[q, 64:128, E : 2 * E] = proj_ref[q]
+        total = total + jnp.dot(got_ref[q], weights[q], preferred_element_type=jnp.float32)
+    both[0] = total[:, 0:E]
+    both[1] = total[:, E : 2 * E]
+    mine_ref[...] = both[zh_ref[0]]
+    other_ref[...] = both[1 - zh_ref[0]]
+
+
+def join_kernel(mine_ref, came_ref, out_ref):
+    emb = (mine_ref[...] + came_ref[...]).astype(jnp.bfloat16)
+    for p in range(out_ref.shape[0]):
+        out_ref[p] = emb
+
+
+def turn_kernel(got_ref, out_ref):
+    for s in range(4):
+        rows = got_ref[s].T
+        for q in range(8):
+            out_ref[q, :, 32 * s : 32 * s + 32] = rows[64 * q : 64 * q + 64]
+
+
+def goods_kernel(got_ref, proj_ref, out_ref):
+    total = jnp.dot(got_ref[0], proj_ref[0], preferred_element_type=jnp.float32)
+    for q in range(1, 8):
+        total = total + jnp.dot(got_ref[q], proj_ref[q], preferred_element_type=jnp.float32)
+    emb = total.astype(jnp.bfloat16)
+    for p in range(out_ref.shape[0]):
+        out_ref[p] = emb
+
+
+def small_call(kernel, outs, *args, scratch=(), smem=0):
+    return pl.pallas_call(
+        kernel,
+        in_specs=[pl.BlockSpec(memory_space=pltpu.SMEM)] * smem + [VM] * (len(args) - smem),
+        out_specs=jax.tree.map(lambda _: VM, outs),
+        out_shape=outs,
+        scratch_shapes=list(scratch),
+        compiler_params=PARAMS,
+    )(*args)
+
+
 def exchange(x, axes):
     return lax.all_to_all(x, axes, 0, 0, tiled=True)
 
 
-def spread_out(x, axes, n):
-    return exchange(jnp.broadcast_to(x[None], (n,) + x.shape), axes)
+def embeddings(buyer_hidden, goods_hidden, buyer_proj, goods_proj, zh):
+    bf16, f32 = jnp.bfloat16, jnp.float32
+    shape = jax.ShapeDtypeStruct
+    goods_part = exchange(goods_hidden.T.reshape(32, 4, 512).transpose(1, 0, 2), ("y",))
+    packed = small_call(pack_kernel, shape((8, 80, 128), bf16), buyer_hidden.T)
+    buyer_part = exchange(packed, ("x", "c"))
+    goods_rows = exchange(small_call(turn_kernel, shape((8, 64, 128), bf16), goods_part), ("zl",))
+    proj = lax.dynamic_index_in_dim(buyer_proj.reshape(4, 2, 2, 64, E), zh, 1, keepdims=False).reshape(8, 64, E)
+    mine, other = small_call(
+        half_kernel, (shape((80, E), f32),) * 2, zh.reshape(1), buyer_part, proj,
+        scratch=(pltpu.VMEM((8, 128, 2 * E), bf16), pltpu.VMEM((2, 80, E), f32)), smem=1,
+    )
+    came = lax.ppermute(other, "zh", [(0, 1), (1, 0)])
+    buyer_emb = exchange(small_call(join_kernel, shape((32, 80, E), bf16), mine, came), PLANE)
+    proj = goods_proj.reshape(4, 8, 32, E).transpose(1, 0, 2, 3).reshape(8, 128, E)
+    goods_emb = exchange(small_call(goods_kernel, shape((16, 64, E), bf16), goods_rows, proj), RING)
+    return buyer_emb.reshape(-1, E), goods_emb.reshape(-1, E)
 
 
 def per_device(buyer_hidden, goods_hidden, buyer_proj, goods_proj, endowment):
     x, y, zh, c = (lax.axis_index(a) for a in ("x", "y", "zh", "c"))
-    rows = lax.all_to_all(buyer_hidden, ("x", "zh", "c"), 0, 1, tiled=True)
-    buyer_own = jnp.dot(rows, buyer_proj, preferred_element_type=jnp.float32).astype(jnp.bfloat16)
-    rows = lax.all_to_all(goods_hidden, ("y", "zl"), 0, 1, tiled=True)
-    goods_own = jnp.dot(rows, goods_proj, preferred_element_type=jnp.float32).astype(jnp.bfloat16)
-    buyer_emb = spread_out(buyer_own, PLANE, 32).reshape(-1, E)
-    goods_emb = spread_out(goods_own, RING, 16).reshape(-1, E)
+    buyer_emb, goods_emb = embeddings(buyer_hidden, goods_hidden, buyer_proj, goods_proj, zh)
 
     mine = lax.dynamic_index_in_dim(endowment.reshape(4, 2, 160), zh, 1, keepdims=False).reshape(5, 128)
     money_row = lax.dynamic_slice(mine, (jnp.minimum(x * 2 + c, 4), 0), (1, 128))
@@ -224,7 +267,7 @@
         sent, before = utility_call(k, ring, values)
         got = exchange(sent, PLANE)
     ring = exchange(price_call(ITERS, got, money, values), RING)
-    final = exchange(utility_call(ITERS, ring, values, before, zh.reshape(1).astype(jnp.int32)), PLANE)
+    final = exchange(utility_call(ITERS, ring, values, before, zh.reshape(1)), PLANE)
     prices = lax.dynamic_index_in_dim(final.reshape(4, 8, LB + 4, 128), x * 2 + c, 1, keepdims=False)[:, LB:].reshape(-1)
     five = lambda a, axis: lax.dynamic_slice_in_dim(a, 5 * y, 5, axis)
     mine_total = jnp.sum(five(final, 1), 0) * five(money, 0) / jnp.sum(five(got, 1), 0)

time: 272 us -> 252 us (0.926)
  waiting for transfers between devices: 71.2 us -> 56.7 us
  Pallas kernels: 36.8 us -> 32.8 us
  local copies, waits for them, and re-layouts: 12.6 us -> 8.92 us
    all_to_all x2 -> x0, starting transfers between devices: 34.3 us -> none  [the longest x1 19.1 us: per_device(): rows = lax.all_to_all(buyer_hidden, ('x', 'zh', 'c'), 0, 1, tiled=True)]
    all_to_all x3 -> x6, starting transfers between devices: 16.4 us -> 44.8 us  [exchange(): return lax.all_to_all(x, axes, 0, 0, tiled=True)]
    all_to_all x2 -> x0, waiting for transfers between devices: 25.7 us -> none  [the longest x1 14.2 us: per_device(): rows = lax.all_to_all(buyer_hidden, ('x', 'zh', 'c'), 0, 1, tiled=True)]
    ppermute x0 -> x1, starting transfers between devices: none -> 7.94 us  [embeddings(): came = lax.ppermute(other, 'zh', [(0, 1), (1, 0)])]
    all_to_all x3 -> x6, waiting for transfers between devices: 36.3 us -> 41.9 us  [exchange(): return lax.all_to_all(x, axes, 0, 0, tiled=True)]
    ppermute x0 -> x1, waiting for transfers between devices: none -> 5.56 us  [embeddings(): came = lax.ppermute(other, 'zh', [(0, 1), (1, 0)])]
    pallas_call x5 -> x10, Pallas kernels: 23.1 us -> 18.6 us  [the longest x3 8.07 us: price_call(): pl.pallas_call(functools.partial(price_kernel, k), in_specs=[VM, VM, VM],...]
    all_to_all x4 -> x0, local copies, waits for them, and re-layouts: 3.41 us -> none  [the longest x2 2.13 us: per_device(): rows = lax.all_to_all(buyer_hidden, ('x', 'zh', 'c'), 0, 1, tiled=True)]
  transfers between devices with their start and end apart: 6 -> 8, of which waited for: 6 -> 7; matrix products, arithmetic and copies ran while one was open for 1% -> 1% of each run, Pallas kernels for 0% -> 2%
where the time goes in v3:
time: 252 us; the launch traced here: 251 us
  blocking collectives  95.6 us (38%)
  waiting for transfers between devices  56.7 us (22%)
  starting transfers between devices  56 us (22%)
  Pallas kernels  32.8 us (13%)
  local copies, waits for them, and re-layouts  8.92 us (4%)
    all_to_all x6, blocking collectives, exchange(): return lax.all_to_all(x, axes, 0, 0, tiled=True)  95.6 us
    all_to_all x6, starting transfers between devices, exchange(): return lax.all_to_all(x, axes, 0, 0, tiled=True)  44.8 us
    all_to_all x6, waiting for transfers between devices, exchange(): return lax.all_to_all(x, axes, 0, 0, tiled=True)  41.9 us
    pallas_call x1, Pallas kernels, values_call(): pl.pallas_call(values_kernel, grid=(GT,), in_specs=[pl.BlockSpec((128, E)...  10.3 us
    ppermute x1, waiting for transfers between devices, per_device(): other = lax.ppermute(mine_total, 'zh', [(0, 1), (1, 0)])  9.23 us
    pallas_call x3, Pallas kernels, price_call(): pl.pallas_call(functools.partial(price_kernel, k), in_specs=[VM, VM, VM],...  8.07 us
    ppermute x1, starting transfers between devices, embeddings(): came = lax.ppermute(other, 'zh', [(0, 1), (1, 0)])  7.94 us
    pallas_call x2, Pallas kernels, utility_call(): pl.pallas_call(functools.partial(utility_kernel, k), in_specs=[VM, VM], o...  6.45 us
  transfers between devices with their start and end apart: 8, of which 7 were waited for; matrix products, arithmetic and copies ran while one was open for 1% of the time, Pallas kernels for 2%

profile of v3, /device:TPU:1, one launch (start us, length us, event | category | flops | bytes accessed | tf_op | source)
XLA Modules:
  0.0 250.9 jit_solution(17782134637890856113)
XLA Ops:
  0.6 0.0 copy-start
  0.6 0.0 copy-start.5
  0.7 1.6 copy.17
  2.3 5.0 %all-to-all-start = ((bf16[4,32,512]{2,1,0:T(8,128)(2,1)}), bf16[4,32,512]{2,1,0:T(8,128)(2,1)S(1)}, u32[]{:S(2)}, u32[]{:S(2)}) async-start(bf16[4,32,512]{2,1,0:T(8,128)(2,1)} %bitcast.24), calls=%async_computation | async-start | bytes 262144 | tf_op jit(solution)/shard_map/all_to_all | solution.py:233
  7.3 0.0 copy-start.2
  7.3 0.9 copy-done.2
  8.2 0.9 shard_map.70
  9.1 3.0 %all-to-all-done.got_ref = bf16[4,32,512]{2,1,0:T(8,128)(2,1)S(1)} async-done(((bf16[4,32,512]{2,1,0:T(8,128)(2,1)}), bf16[4,32,512]{2,1,0:T(8,128)(2,1)S(1)}, u32[]{:S(2)}, u32[]{:S(2)}) %all-to-all-start) | async-done | bytes 131104 | tf_op jit(solution)/shard_map/all_to_all | solution.py:233
  12.1 9.6 %all-to-all-start.3 = ((bf16[8,80,128]{2,1,0:T(8,128)(2,1)}), bf16[8,80,128]{2,1,0:T(8,128)(2,1)S(1)}, u32[]{:S(2)}, u32[]{:S(2)}) async-start(bf16[8,80,128]{2,1,0:T(8,128)(2,1)} %shard_map.70), calls=%async_computation.3 | async-start | bytes 327680 | tf_op jit(solution)/shard_map/all_to_all | solution.py:233
  21.7 1.1 shard_map.68
  22.7 4.5 %all-to-all-done.3.got_ref = bf16[8,80,128]{2,1,0:T(8,128)(2,1)S(1)} async-done(((bf16[8,80,128]{2,1,0:T(8,128)(2,1)}), bf16[8,80,128]{2,1,0:T(8,128)(2,1)S(1)}, u32[]{:S(2)}, u32[]{:S(2)}) %all-to-all-start.3) | async-done | bytes 163872 | tf_op jit(solution)/shard_map/all_to_all | solution.py:233
  27.2 9.1 %all-to-all-start.1 = ((bf16[8,64,128]{2,1,0:T(8,128)(2,1)}), bf16[8,64,128]{2,1,0:T(8,128)(2,1)S(1)}, u32[]{:S(2)}, u32[]{:S(2)}) async-start(bf16[8,64,128]{2,1,0:T(8,128)(2,1)} %shard_map.68), calls=%async_computation.1 | async-start | bytes 262144 | tf_op jit(solution)/shard_map/all_to_all | solution.py:233
  36.3 0.0 copy-done
  36.3 0.3 shard_map.71
  36.6 7.9 %collective-permute-start = (f32[80,128]{1,0:T(8,128)S(1)}, f32[80,128]{1,0:T(8,128)S(1)}, u32[]{:S(2)}, u32[]{:S(2)}) collective-permute-start(f32[80,128]{1,0:T(8,128)S(1)} %get-tuple-element.10), channel_id=1, source_target_pairs={{0,2},{2,0},{1,3},{3,1},{4,6},{6,4},{5,7},{7,5},{8,10},{10,8},{9,1... | collective-permute-start | bytes 122888 | tf_op jit(solution)/shard_map/ppermute | solution.py:248
  44.6 5.6 %collective-permute-done.came_ref = f32[80,128]{1,0:T(8,128)S(1)} collective-permute-done((f32[80,128]{1,0:T(8,128)S(1)}, f32[80,128]{1,0:T(8,128)S(1)}, u32[]{:S(2)}, u32[]{:S(2)}) %collective-permute-start) | collective-permute-done | bytes 40992 | tf_op jit(solution)/shard_map/ppermute | solution.py:248
  50.1 0.9 shard_map.72
  51.0 0.0 all-to-all-done.1.got_ref
  51.0 5.8 %all-to-all-start.4 = ((bf16[32,80,128]{2,1,0:T(8,128)(2,1)}), bf16[32,80,128]{2,1,0:T(8,128)(2,1)S(1)}, u32[]{:S(2)}, u32[]{:S(2)}) async-start(bf16[32,80,128]{2,1,0:T(8,128)(2,1)} %shard_map.72), calls=%async_computation.4 | async-start | bytes 1310720 | tf_op jit(solution)/shard_map/all_to_all | solution.py:233
  56.9 1.0 copy.10
  57.9 0.9 shard_map.69
  58.8 11.0 %all-to-all-done.4 = bf16[32,80,128]{2,1,0:T(8,128)(2,1)S(1)} async-done(((bf16[32,80,128]{2,1,0:T(8,128)(2,1)}), bf16[32,80,128]{2,1,0:T(8,128)(2,1)S(1)}, u32[]{:S(2)}, u32[]{:S(2)}) %all-to-all-start.4) | async-done | bytes 655392 | tf_op jit(solution)/shard_map/all_to_all | solution.py:233
  69.8 0.0 copy-start.3
  69.8 9.7 %all-to-all-start.2 = ((bf16[16,64,128]{2,1,0:T(8,128)(2,1)}), bf16[16,64,128]{2,1,0:T(8,128)(2,1)S(1)}, u32[]{:S(2)}, u32[]{:S(2)}) async-start(bf16[16,64,128]{2,1,0:T(8,128)(2,1)} %shard_map.69), calls=%async_computation.2 | async-start | bytes 524288 | tf_op jit(solution)/shard_map/all_to_all | solution.py:233
  79.6 0.0 copy-done.5
  79.6 0.1 reshape.57
  79.7 0.1 reshape.58
  79.8 0.5 constant_dynamic-slice_fusion.money_ref
  80.3 13.1 %all-to-all-done.2 = bf16[16,64,128]{2,1,0:T(8,128)(2,1)S(1)} async-done(((bf16[16,64,128]{2,1,0:T(8,128)(2,1)}), bf16[16,64,128]{2,1,0:T(8,128)(2,1)S(1)}, u32[]{:S(2)}, u32[]{:S(2)}) %all-to-all-start.2) | async-done | bytes 262176 | tf_op jit(solution)/shard_map/all_to_all | solution.py:233
  93.4 0.0 copy-start.4
  93.4 0.0 copy-done.3
  93.4 0.7 copy-done.4
  94.1 10.3 %shard_map.73 = (bf16[1024,2560]{1,0:T(8,128)(2,1)}, f32[32,21,128]{2,1,0:T(8,128)}) custom-call(bf16[1024,128]{1,0:T(8,128)(2,1)} %bitcast.33, bf16[2560,128]{1,0:T(8,128)(2,1)} %bitcast.32, f32[1,128]{1,0:T(1,128)} %constant_dynamic-slice_fusion.money_ref), custom_call_target="tpu_custom_call" | custom-call | tf_op jit(solution)/shard_map/pallas_call | solution.py:122
  104.4 19.1 %all_to_all.60.got_ref = f32[32,21,128]{2,1,0:T(8,128)S(1)} all-to-all(f32[32,21,128]{2,1,0:T(8,128)} %get-tuple-element.11), channel_id=1, replica_groups=mesh['y'=4,'zl'=8,'x'=4,'zh'=2,'c'=2] {'y','x','c'}, dimensions={0} | all-to-all | bytes 688128 | tf_op jit(solution)/shard_map/all_to_all | solution.py:233
  123.5 0.0 copy-start.1
  123.5 2.5 copy-done.1
  126.0 2.4 shard_map.74
  128.4 17.1 %all_to_all.61.got_ref = f32[16,8,128]{2,1,0:T(8,128)S(1)} all-to-all(f32[16,8,128]{2,1,0:T(8,128)S(1)} %shard_map.74), channel_id=1, replica_groups=mesh['y'=4,'zl'=8,'x'=4,'zh'=2,'c'=2] {'zh','zl'}, dimensions={0} | all-to-all | bytes 131072 | tf_op jit(solution)/shard_map/all_to_all | solution.py:233
  145.5 3.3 %shard_map.75 = (f32[32,20,128]{2,1,0:T(8,128)S(1)}, f32[8,128]{1,0:T(8,128)}) custom-call(f32[16,8,128]{2,1,0:T(8,128)S(1)} %all_to_all.61.got_ref, bf16[1024,2560]{1,0:T(8,128)(2,1)S(1)} %copy-done.1), custom_call_target="tpu_custom_call" | custom-call | tf_op jit(solution)/shard_map/pallas_call | solution.py:169
  148.8 15.4 %all_to_all.62.got_ref = f32[32,20,128]{2,1,0:T(8,128)S(1)} all-to-all(f32[32,20,128]{2,1,0:T(8,128)S(1)} %get-tuple-element.13), channel_id=1, replica_groups=mesh['y'=4,'zl'=8,'x'=4,'zh'=2,'c'=2] {'y','x','c'}, dimensions={0} | all-to-all | bytes 655360 | tf_op jit(solution)/shard_map/all_to_all | solution.py:233
  164.2 0.0 slice-start
  164.2 2.7 %shard_map.76 = f32[16,8,128]{2,1,0:T(8,128)S(1)} custom-call(f32[32,20,128]{2,1,0:T(8,128)S(1)} %all_to_all.62.got_ref, f32[20,128]{1,0:T(8,128)S(1)} %reshape.59.money_ref, bf16[1024,2560]{1,0:T(8,128)(2,1)S(1)} %copy-done.1), custom_call_target="tpu_custom_call" | custom-call | tf_op jit(solution)/shard_map/pallas_call | solution.py:144
  166.9 14.3 %all_to_all.63.got_ref = f32[16,8,128]{2,1,0:T(8,128)S(1)} all-to-all(f32[16,8,128]{2,1,0:T(8,128)S(1)} %shard_map.76), channel_id=1, replica_groups=mesh['y'=4,'zl'=8,'x'=4,'zh'=2,'c'=2] {'zh','zl'}, dimensions={0} | all-to-all | bytes 131072 | tf_op jit(solution)/shard_map/all_to_all | solution.py:233
  181.2 0.0 slice-start.1
  181.2 3.1 %shard_map.77 = (f32[32,20,128]{2,1,0:T(8,128)S(1)}, f32[8,128]{1,0:T(8,128)S(1)}) custom-call(f32[16,8,128]{2,1,0:T(8,128)S(1)} %all_to_all.63.got_ref, bf16[1024,2560]{1,0:T(8,128)(2,1)S(1)} %copy-done.1), custom_call_target="tpu_custom_call" | custom-call | tf_op jit(solution)/shard_map/pallas_call | solution.py:169
  184.4 15.4 %all_to_all.64.got_ref = f32[32,20,128]{2,1,0:T(8,128)S(1)} all-to-all(f32[32,20,128]{2,1,0:T(8,128)S(1)} %get-tuple-element.14), channel_id=1, replica_groups=mesh['y'=4,'zl'=8,'x'=4,'zh'=2,'c'=2] {'y','x','c'}, dimensions={0} | all-to-all | bytes 655360 | tf_op jit(solution)/shard_map/all_to_all | solution.py:233
  199.8 3.0 %shard_map.78 = f32[16,8,128]{2,1,0:T(8,128)S(1)} custom-call(f32[32,20,128]{2,1,0:T(8,128)S(1)} %all_to_all.64.got_ref, f32[20,128]{1,0:T(8,128)S(1)} %reshape.59.money_ref, bf16[1024,2560]{1,0:T(8,128)(2,1)S(1)} %copy-done.1), custom_call_target="tpu_custom_call" | custom-call | tf_op jit(solution)/shard_map/pallas_call | solution.py:144
  202.8 14.3 %all_to_all.65.got_ref = f32[16,8,128]{2,1,0:T(8,128)S(1)} all-to-all(f32[16,8,128]{2,1,0:T(8,128)S(1)} %shard_map.78), channel_id=1, replica_groups=mesh['y'=4,'zl'=8,'x'=4,'zh'=2,'c'=2] {'zh','zl'}, dimensions={0} | all-to-all | bytes 131072 | tf_op jit(solution)/shard_map/all_to_all | solution.py:233
  217.1 0.0 slice-done
  217.1 0.0 slice-done.1
  217.1 3.9 %shard_map.79 = f32[32,24,128]{2,1,0:T(8,128)} custom-call(f32[16,8,128]{2,1,0:T(8,128)S(1)} %all_to_all.65.got_ref, f32[8,128]{1,0:T(8,128)S(1)} %get-tuple-element.15.refs_0_, s32[1]{0:T(128)} %bitcast.6.zh_ref.refs_1_, bf16[1024,2560]{1,0:T(8,128)(2,1)S(1)} %bitcast.28), custom_call_target="tpu_custom_call" | custom-call | tf_op jit(solution)/shard_map/pallas_call | solution.py:161
  221.0 5.7 %all-to-all-start.11 = ((f32[32,24,128]{2,1,0:T(8,128)}), f32[32,24,128]{2,1,0:T(8,128)S(1)}, u32[]{:S(2)}, u32[]{:S(2)}) async-start(f32[32,24,128]{2,1,0:T(8,128)} %shard_map.79), calls=%async_computation.11 | async-start | bytes 786432 | tf_op jit(solution)/shard_map/all_to_all | solution.py:233
  226.7 10.2 %all-to-all-done.11 = f32[32,24,128]{2,1,0:T(8,128)S(1)} async-done(((f32[32,24,128]{2,1,0:T(8,128)}), f32[32,24,128]{2,1,0:T(8,128)S(1)}, u32[]{:S(2)}, u32[]{:S(2)}) %all-to-all-start.11) | async-done | bytes 393248 | tf_op jit(solution)/shard_map/all_to_all | solution.py:233
  237.0 3.2 %collective-permute-start.1 = (f32[5,128]{1,0:T(8,128)S(1)}, f32[5,128]{1,0:T(8,128)S(1)}, u32[]{:S(2)}, u32[]{:S(2)}) collective-permute-start(f32[5,128]{1,0:T(8,128)S(1)} %multiply_divide_fusion), channel_id=1, source_target_pairs={{0,2},{2,0},{1,3},{3,1},{4,6},{6,4},{5,7},{7,5},{8,10},{10,8},{9,1... | collective-permute-start | bytes 7688 | tf_op jit(solution)/shard_map/ppermute | solution.py:274
  240.2 0.6 slice.14
  240.8 9.2 %collective-permute-done.1 = f32[5,128]{1,0:T(8,128)S(1)} collective-permute-done((f32[5,128]{1,0:T(8,128)S(1)}, f32[5,128]{1,0:T(8,128)S(1)}, u32[]{:S(2)}, u32[]{:S(2)}) %collective-permute-start.1) | collective-permute-done | bytes 2592 | tf_op jit(solution)/shard_map/ppermute | solution.py:274
  250.1 0.1 stack_reshape.8
  250.1 0.1 stack_reshape.9
  250.2 0.7 reshape.62
  (11 shorter events, 0.2 us)
Async XLA Ops:
  0.6 35.7 %copy-start = (bf16[1024,128]{1,0:T(8,128)(2,1)S(1)}, bf16[1024,128]{1,0:T(8,128)(2,1)}, u32[]{:S(2)}) copy-start(bf16[1024,128]{1,0:T(8,128)(2,1)} %param.7) | copy-start | bytes 786436
  0.6 78.9 %copy-start.5 = (f32[1280]{0:T(1024)S(1)}, f32[1280]{0:T(1024)}, u32[]{:S(2)}) copy-start(f32[1280]{0:T(1024)} %param.9) | copy-start | bytes 15364
  2.3 9.8 %all-to-all-start = ((bf16[4,32,512]{2,1,0:T(8,128)(2,1)}), bf16[4,32,512]{2,1,0:T(8,128)(2,1)S(1)}, u32[]{:S(2)}, u32[]{:S(2)}) async-start(bf16[4,32,512]{2,1,0:T(8,128)(2,1)} %bitcast.24), calls=%async_computation | async-start | bytes 262144 | tf_op jit(solution)/shard_map/all_to_all | solution.py:233
  7.3 0.9 copy-start.2
  12.1 15.1 %all-to-all-start.3 = ((bf16[8,80,128]{2,1,0:T(8,128)(2,1)}), bf16[8,80,128]{2,1,0:T(8,128)(2,1)S(1)}, u32[]{:S(2)}, u32[]{:S(2)}) async-start(bf16[8,80,128]{2,1,0:T(8,128)(2,1)} %shard_map.70), calls=%async_computation.3 | async-start | bytes 327680 | tf_op jit(solution)/shard_map/all_to_all | solution.py:233
  27.2 23.8 %all-to-all-start.1 = ((bf16[8,64,128]{2,1,0:T(8,128)(2,1)}), bf16[8,64,128]{2,1,0:T(8,128)(2,1)S(1)}, u32[]{:S(2)}, u32[]{:S(2)}) async-start(bf16[8,64,128]{2,1,0:T(8,128)(2,1)} %shard_map.68), calls=%async_computation.1 | async-start | bytes 262144 | tf_op jit(solution)/shard_map/all_to_all | solution.py:233
  36.6 13.5 %collective-permute-start = (f32[80,128]{1,0:T(8,128)S(1)}, f32[80,128]{1,0:T(8,128)S(1)}, u32[]{:S(2)}, u32[]{:S(2)}) collective-permute-start(f32[80,128]{1,0:T(8,128)S(1)} %get-tuple-element.10), channel_id=1, source_target_pairs={{0,2},{2,0},{1,3},{3,1},{4,6},{6,4},{5,7},{7,5},{8,10},{10,8},{9,1... | collective-permute-start | bytes 122888 | tf_op jit(solution)/shard_map/ppermute | solution.py:248
  51.0 18.8 %all-to-all-start.4 = ((bf16[32,80,128]{2,1,0:T(8,128)(2,1)}), bf16[32,80,128]{2,1,0:T(8,128)(2,1)S(1)}, u32[]{:S(2)}, u32[]{:S(2)}) async-start(bf16[32,80,128]{2,1,0:T(8,128)(2,1)} %shard_map.72), calls=%async_computation.4 | async-start | bytes 1310720 | tf_op jit(solution)/shard_map/all_to_all | solution.py:233
  69.8 23.6 %copy-start.3 = (bf16[32,80,128]{2,1,0:T(8,128)(2,1)}, bf16[32,80,128]{2,1,0:T(8,128)(2,1)S(1)}, u32[]{:S(2)}) copy-start(bf16[32,80,128]{2,1,0:T(8,128)(2,1)S(1)} %all-to-all-done.4) | copy-start | bytes 1966084
  69.8 23.6 %all-to-all-start.2 = ((bf16[16,64,128]{2,1,0:T(8,128)(2,1)}), bf16[16,64,128]{2,1,0:T(8,128)(2,1)S(1)}, u32[]{:S(2)}, u32[]{:S(2)}) async-start(bf16[16,64,128]{2,1,0:T(8,128)(2,1)} %shard_map.69), calls=%async_computation.2 | async-start | bytes 524288 | tf_op jit(solution)/shard_map/all_to_all | solution.py:233
  93.4 0.7 copy-start.4
  123.5 2.5 copy-start.1
  164.2 52.9 %slice-start = ((s8[5242880]{0:T(1024)(128)(4,1)}), s8[4194304]{0:T(1024)(128)(4,1)S(1)}, s32[]{:S(2)}) async-start(s8[5242880]{0:T(1024)(128)(4,1)} %bitcast.27), calls=%async_computation.12 | async-start | bytes 8388608
  181.2 35.9 %slice-start.1 = ((s8[5242880]{0:T(1024)(128)(4,1)}), s8[1048576]{0:T(1024)(128)(4,1)S(1)}, s32[]{:S(2)}) async-start(s8[5242880]{0:T(1024)(128)(4,1)} %bitcast.27), calls=%async_computation.13 | async-start | bytes 2097152
  221.0 15.9 %all-to-all-start.11 = ((f32[32,24,128]{2,1,0:T(8,128)}), f32[32,24,128]{2,1,0:T(8,128)S(1)}, u32[]{:S(2)}, u32[]{:S(2)}) async-start(f32[32,24,128]{2,1,0:T(8,128)} %shard_map.79), calls=%async_computation.11 | async-start | bytes 786432 | tf_op jit(solution)/shard_map/all_to_all | solution.py:233
  237.0 13.1 %collective-permute-start.1 = (f32[5,128]{1,0:T(8,128)S(1)}, f32[5,128]{1,0:T(8,128)S(1)}, u32[]{:S(2)}, u32[]{:S(2)}) collective-permute-start(f32[5,128]{1,0:T(8,128)S(1)} %multiply_divide_fusion), channel_id=1, source_target_pairs={{0,2},{2,0},{1,3},{3,1},{4,6},{6,4},{5,7},{7,5},{8,10},{10,8},{9,1... | collective-permute-start | bytes 7688 | tf_op jit(solution)/shard_map/ppermute | solution.py:274
